TPU v7x, 512 devices: a whole 4x8x8 slice. The times are simulated.
512 devices in a mesh: row: 32 (over y, x), col: 16 (over z, core).
Axes of the slice: x: 4, y: 8, z: 8, core: 2. Of those that a mesh axis runs over, the one named last changes fastest.
Arguments:
- activations: bfloat16 [384, 8192], P('row', 'col'), may hold values from -6 to 6
- gate_weight: bfloat16 [8192, 16384], P('col', 'row'), may hold values from -0.0625 to 0.0625
- up_weight: bfloat16 [8192, 16384], P('col', 'row'), may hold values from -0.0625 to 0.0625
- down_weight: bfloat16 [16384, 8192], P('row', 'col'), may hold values from -0.046875 to 0.046875
- out_grad: bfloat16 [384, 8192], P('row', 'col'), may hold values from -1.75 to 1.75
Outputs:
- layer_out: bfloat16 [384, 8192], P('row', 'col')
- input_grad: bfloat16 [384, 8192], P('row', 'col')
- gate_grad: float32 [8192, 16384], P('col', 'row')
- up_grad: float32 [8192, 16384], P('col', 'row')
- down_grad: float32 [16384, 8192], P('row', 'col')
All inputs are finite; a program needn't handle non-finite values.
Results may differ from a plain program's by a relative error of at most 0.005.
Values may be sent and summed in bfloat16 or wider, within the bound.
No kernel may reach another device: no remote copies, remote signals or barrier semaphores. Data moves between devices by JAX's collectives and lax.ppermute only.
A program may use at most 64 MiB of HBM per device.

v0:
```python
import jax
import jax.numpy as jnp
from jax import lax
from jax.sharding import PartitionSpec as P


def contract_rows(left_side, right_side):
    return lax.dot_general(
        left_side, right_side, (((0,), (0,)), ((), ())), preferred_element_type=jnp.float32
    )


def contract_cols(left_side, right_side):
    return lax.dot_general(
        left_side, right_side, (((1,), (1,)), ((), ())), preferred_element_type=jnp.float32
    )


def swiglu_deltas(hidden_grad, gate, up):
    gate_sigmoid = jax.nn.sigmoid(gate)
    gate_silu = gate * gate_sigmoid
    gate_delta = (hidden_grad * up * gate_sigmoid * (1.0 + gate * (1.0 - gate_sigmoid))).astype(
        jnp.bfloat16
    )
    up_delta = (hidden_grad * gate_silu).astype(jnp.bfloat16)
    return (gate_delta, up_delta)


def local(activations, gate_weight, up_weight, down_weight, out_grad):
    hidden_width = gate_weight.shape[1]
    feature_width = activations.shape[1]
    all_tokens, all_grads = (
        lax.all_gather(activations, "row", axis=0, tiled=True),
        lax.all_gather(out_grad, "row", axis=0, tiled=True),
    )
    both_weights = jnp.concatenate([gate_weight, up_weight], axis=1)
    picked = all_tokens
    summed = lax.psum_scatter(
        jnp.dot(picked, both_weights, preferred_element_type=jnp.float32),
        "col",
        scatter_dimension=0,
        tiled=True,
    )
    gate = summed[:, :hidden_width]
    up = summed[:, hidden_width:]
    hidden = (jax.nn.silu(gate) * up).astype(jnp.bfloat16)
    hidden_all = lax.all_gather(hidden, "col", axis=0, tiled=True)
    picked = all_grads
    hidden_grad = lax.psum_scatter(
        contract_cols(picked, down_weight), "col", scatter_dimension=0, tiled=True
    )
    gate_delta, up_delta = swiglu_deltas(hidden_grad, gate, up)
    all_gate_delta, all_up_delta = (
        lax.all_gather(gate_delta, "col", axis=0, tiled=True),
        lax.all_gather(up_delta, "col", axis=0, tiled=True),
    )
    gate_grad = contract_rows(all_tokens, all_gate_delta)
    up_grad = contract_rows(all_tokens, all_up_delta)
    down_grad = contract_rows(hidden_all, all_grads)
    forward_term = jnp.dot(hidden_all, down_weight, preferred_element_type=jnp.float32)
    backward_term = contract_cols(all_gate_delta, gate_weight) + contract_cols(
        all_up_delta, up_weight
    )
    row_total = lax.psum_scatter(
        jnp.concatenate([forward_term, backward_term], axis=1),
        "row",
        scatter_dimension=0,
        tiled=True,
    )
    layer_out = row_total[:, :feature_width].astype(jnp.bfloat16)
    input_grad = row_total[:, feature_width:].astype(jnp.bfloat16)
    return (layer_out, input_grad, gate_grad, up_grad, down_grad)


def solution(mesh):
    return jax.shard_map(
        local,
        mesh=mesh,
        in_specs=(
            P("row", "col"),
            P("col", "row"),
            P("col", "row"),
            P("row", "col"),
            P("row", "col"),
        ),
        out_specs=(
            P("row", "col"),
            P("row", "col"),
            P("col", "row"),
            P("col", "row"),
            P("row", "col"),
        ),
        check_vma=False,
    )
```

profile of v0, /device:TPU:64, one launch (start us, length us, event | category | flops | bytes accessed | tf_op | source)
XLA Modules:
  0.0 370.0 jit_solution(8546678322941645992)
XLA Ops:
  7.2 50.6 %all-gather.1 = bf16[32,12,512]{2,1,0:T(8,128)(2,1)S(1)} all-gather(bf16[1,12,512]{2,1,0:T(8,128)(2,1)} %bitcast.28), channel_id=1, replica_groups=mesh['row'=32,'col'=16] {'row'}, dimensions={0}, use_global_device_ids=true | all-gather | bytes 405504 | tf_op jit(solution)/shard_map/all_gather | solution.py:34
  58.0 1.3 fusion.9
  59.3 48.1 %all-gather = bf16[32,12,512]{2,1,0:T(8,128)(2,1)S(1)} all-gather(bf16[1,12,512]{2,1,0:T(8,128)(2,1)S(1)} %bitcast.29), channel_id=1, replica_groups=mesh['row'=32,'col'=16] {'row'}, dimensions={0}, use_global_device_ids=true | all-gather | bytes 405504 | tf_op jit(solution)/shard_map/all_gather | solution.py:33
  107.6 1.8 convolution_bitcast_fusion
  109.4 1.6 copy.30
  111.1 1.3 dynamic-slice.4
  113.0 4.8 %reduce-scatter.11.cloned.1.call-done = f32[24,512]{1,0:T(8,128)} async-done(((f32[384,512]{1,0:T(8,128)}), f32[24,512]{1,0:T(8,128)}) %reduce-scatter.11.cloned.1.call-update) | async-done | bytes 49168 | tf_op jit(solution)/shard_map/reduce_scatter | solution.py:49
  117.9 62.4 %reduce-scatter.9.cloned.1.call-done = f32[24,1024]{1,0:T(8,128)} async-done(((f32[384,1024]{1,0:T(8,128)}), f32[24,1024]{1,0:T(8,128)}) %reduce-scatter.9.cloned.1.call-update) | async-done | bytes 98320 | tf_op jit(solution)/shard_map/reduce_scatter | solution.py:38
  180.2 0.9 multiply_convert_fusion
  181.1 18.8 %all_gather.18 = bf16[384,512]{1,0:T(8,128)(2,1)S(1)} all-gather(bf16[24,512]{1,0:T(8,128)(2,1)S(1)} %get-tuple-element.26), channel_id=1, replica_groups=mesh['row'=32,'col'=16] {'col'}, dimensions={0}, use_global_device_ids=true | all-gather | bytes 417792 | tf_op jit(solution)/shard_map/all_gather | solution.py:54
  199.9 0.4 fusion.10
  200.3 15.4 %all_gather.19 = bf16[384,512]{1,0:T(8,128)(2,1)S(1)} all-gather(bf16[24,512]{1,0:T(8,128)(2,1)S(1)} %get-tuple-element.25), channel_id=1, replica_groups=mesh['row'=32,'col'=16] {'col'}, dimensions={0}, use_global_device_ids=true | all-gather | bytes 417792 | tf_op jit(solution)/shard_map/all_gather | solution.py:55
  215.8 17.1 %all_gather.16 = bf16[384,512]{1,0:T(8,128)(2,1)S(1)} all-gather(bf16[24,512]{1,0:T(8,128)(2,1)S(1)} %get-tuple-element.27), channel_id=1, replica_groups=mesh['row'=32,'col'=16] {'col'}, dimensions={0}, use_global_device_ids=true | all-gather | bytes 417792 | tf_op jit(solution)/shard_map/all_gather | solution.py:47
  233.2 0.4 copy-done.3
  233.6 0.4 convolution_add_fusion
  234.2 88.3 %fusion = f32[16,1024]{1,0:T(8,128)S(1)} fusion(f32[384,1024]{1,0:T(8,128)S(1)} %pad_maximum_fusion), kind=kCustom, calls=%all-reduce-scatter | all-reduce-scatter fusion | flops 524289 | bytes 1640448
  322.4 1.3 collective-permute-start
  323.7 1.3 collective-permute-start.1
  325.0 1.9 collective-permute-start.2
  326.9 1.9 collective-permute-start.3
  328.9 0.5 convolution_bitcast_fusion.2
  329.3 10.8 %collective-permute-start.7 = (bf16[12,1024]{1,0:T(8,128)(2,1)S(1)}, bf16[12,1024]{1,0:T(8,128)(2,1)S(1)}, u32[]{:S(2)}, u32[]{:S(2)}) collective-permute-start(bf16[12,1024]{1,0:T(8,128)(2,1)S(1)} %slice.22), channel_id=1, source_target_pairs={{0,128},{16,144},{32,160},{48,176},{64,192},{80,208},{96,224},{112... | collective-permute-start | bytes 73736
  340.1 0.5 convolution_bitcast_fusion.1
  340.6 1.1 collective-permute-done.7
  341.7 2.2 collective-permute-start.4
  343.9 6.0 %collective-permute-start.5 = (bf16[16,1024]{1,0:T(8,128)(2,1)S(1)}, bf16[16,1024]{1,0:T(8,128)(2,1)S(1)}, u32[]{:S(2)}, u32[]{:S(2)}) collective-permute-start(bf16[16,1024]{1,0:T(8,128)(2,1)S(1)} %convert.20), channel_id=1, source_target_pairs={{0,96},{16,112},{32,128},{48,144},{64,160},{80,176},{96,192},{112,... | collective-permute-start | bytes 98312
  350.0 5.8 %collective-permute-start.6 = (bf16[16,1024]{1,0:T(8,128)(2,1)S(1)}, bf16[16,1024]{1,0:T(8,128)(2,1)S(1)}, u32[]{:S(2)}, u32[]{:S(2)}) collective-permute-start(bf16[16,1024]{1,0:T(8,128)(2,1)S(1)} %convert.20), channel_id=1, source_target_pairs={{0,112},{16,128},{32,144},{48,160},{64,176},{80,192},{96,208},{112... | collective-permute-start | bytes 98312
  355.8 1.4 fusion.11
  357.2 1.3 copy.27
  358.6 1.3 copy.28
  359.9 2.6 concatenate.8
  362.5 0.6 fusion.7
  (43 shorter events, 0.9 us)
Async XLA Ops:
  7.2 50.8 %copy-start = (bf16[512,512]{1,0:T(8,128)(2,1)S(1)}, bf16[512,512]{1,0:T(8,128)(2,1)}, u32[]{:S(2)}) copy-start(bf16[512,512]{1,0:T(8,128)(2,1)} %param.8) | copy-start | bytes 1572868
  7.2 110.7 %reduce-scatter.11.cloned.1.call-start = ((), (), s32[]{:S(2)}) async-start(), calls=%async_computation.3 | async-start | bytes 835584 | tf_op jit(solution)/shard_map/reduce_scatter | solution.py:49
  57.8 1.5 copy-start.12
  57.9 49.6 %copy-start.1 = (bf16[384,512]{1,0:T(8,128)(2,1)}, bf16[384,512]{1,0:T(8,128)(2,1)S(1)}, u32[]{:S(2)}) copy-start(bf16[384,512]{1,0:T(8,128)(2,1)S(1)} %reshape.13) | copy-start | bytes 1179652
  57.9 49.6 %copy-start.5 = (bf16[512,512]{1,0:T(8,128)(2,1)S(1)}, bf16[512,512]{1,0:T(8,128)(2,1)}, u32[]{:S(2)}) copy-start(bf16[512,512]{1,0:T(8,128)(2,1)} %param.7) | copy-start | bytes 1572868
  59.3 121.0 %reduce-scatter.9.cloned.1.call-start = ((), (), s32[]{:S(2)}) async-start(), calls=%async_computation.2 | async-start | bytes 1671168 | tf_op jit(solution)/shard_map/reduce_scatter | solution.py:38
  111.0 88.9 %copy-start.7 = (bf16[512,512]{1,0:T(8,128)(2,1)S(1)}, bf16[512,512]{1,0:T(8,128)(2,1)}, u32[]{:S(2)}) copy-start(bf16[512,512]{1,0:T(8,128)(2,1)} %param.6) | copy-start | bytes 1572868
  200.3 33.3 %copy-start.6 = (bf16[512,512]{1,0:T(8,128)(2,1)S(1)}, bf16[512,512]{1,0:T(8,128)(2,1)}, u32[]{:S(2)}) copy-start(bf16[512,512]{1,0:T(8,128)(2,1)} %param.7) | copy-start | bytes 1572868
  232.9 0.7 copy-start.3
  322.4 21.5 %collective-permute-start = (bf16[16,1024]{1,0:T(8,128)(2,1)S(1)}, bf16[16,1024]{1,0:T(8,128)(2,1)S(1)}, u32[]{:S(2)}, u32[]{:S(2)}) collective-permute-start(bf16[16,1024]{1,0:T(8,128)(2,1)S(1)} %convert.20), channel_id=1, source_target_pairs={{0,16},{16,32},{32,48},{48,64},{64,80},{80,96},{96,112},{112,128},... | collective-permute-start | bytes 98312
  323.7 26.2 %collective-permute-start.1 = (bf16[16,1024]{1,0:T(8,128)(2,1)S(1)}, bf16[16,1024]{1,0:T(8,128)(2,1)S(1)}, u32[]{:S(2)}, u32[]{:S(2)}) collective-permute-start(bf16[16,1024]{1,0:T(8,128)(2,1)S(1)} %convert.20), channel_id=1, source_target_pairs={{0,32},{16,48},{32,64},{48,80},{64,96},{80,112},{96,128},{112,144}... | collective-permute-start | bytes 98312
  325.0 34.8 %collective-permute-start.2 = (bf16[16,1024]{1,0:T(8,128)(2,1)S(1)}, bf16[16,1024]{1,0:T(8,128)(2,1)}, u32[]{:S(2)}, u32[]{:S(2)}) collective-permute-start(bf16[16,1024]{1,0:T(8,128)(2,1)S(1)} %convert.20), channel_id=1, source_target_pairs={{0,48},{16,64},{32,80},{48,96},{64,112},{80,128},{96,144},{112,160... | collective-permute-start | bytes 98312
  326.9 32.9 %collective-permute-start.3 = (bf16[16,1024]{1,0:T(8,128)(2,1)S(1)}, bf16[16,1024]{1,0:T(8,128)(2,1)}, u32[]{:S(2)}, u32[]{:S(2)}) collective-permute-start(bf16[16,1024]{1,0:T(8,128)(2,1)S(1)} %convert.20), channel_id=1, source_target_pairs={{0,64},{16,80},{32,96},{48,112},{64,128},{80,144},{96,160},{112,17... | collective-permute-start | bytes 98312
  328.8 27.0 %copy-start.2 = (bf16[384,512]{1,0:T(8,128)(2,1)S(1)}, bf16[384,512]{1,0:T(8,128)(2,1)}, u32[]{:S(2)}) copy-start(bf16[384,512]{1,0:T(8,128)(2,1)} %copy-done.1) | copy-start | bytes 1179652
  328.9 27.0 %copy-start.4 = (bf16[384,512]{1,0:T(8,128)(2,1)S(1)}, bf16[384,512]{1,0:T(8,128)(2,1)}, u32[]{:S(2)}) copy-start(bf16[384,512]{1,0:T(8,128)(2,1)} %copy-done.3) | copy-start | bytes 1179652
  329.3 12.4 %collective-permute-start.7 = (bf16[12,1024]{1,0:T(8,128)(2,1)S(1)}, bf16[12,1024]{1,0:T(8,128)(2,1)S(1)}, u32[]{:S(2)}, u32[]{:S(2)}) collective-permute-start(bf16[12,1024]{1,0:T(8,128)(2,1)S(1)} %slice.22), channel_id=1, source_target_pairs={{0,128},{16,144},{32,160},{48,176},{64,192},{80,208},{96,224},{112... | collective-permute-start | bytes 73736
  341.7 14.1 %copy-start.10 = (bf16[12,1024]{1,0:T(8,128)(2,1)}, bf16[12,1024]{1,0:T(8,128)(2,1)S(1)}, u32[]{:S(2)}) copy-start(bf16[12,1024]{1,0:T(8,128)(2,1)S(1)} %collective-permute-done.7) | copy-start | bytes 73732
  341.7 18.2 %collective-permute-start.4 = (bf16[16,1024]{1,0:T(8,128)(2,1)S(1)}, bf16[16,1024]{1,0:T(8,128)(2,1)S(1)}, u32[]{:S(2)}, u32[]{:S(2)}) collective-permute-start(bf16[16,1024]{1,0:T(8,128)(2,1)S(1)} %convert.20), channel_id=1, source_target_pairs={{0,80},{16,96},{32,112},{48,128},{64,144},{80,160},{96,176},{112,1... | collective-permute-start | bytes 98312
  343.9 15.9 %collective-permute-start.5 = (bf16[16,1024]{1,0:T(8,128)(2,1)S(1)}, bf16[16,1024]{1,0:T(8,128)(2,1)S(1)}, u32[]{:S(2)}, u32[]{:S(2)}) collective-permute-start(bf16[16,1024]{1,0:T(8,128)(2,1)S(1)} %convert.20), channel_id=1, source_target_pairs={{0,96},{16,112},{32,128},{48,144},{64,160},{80,176},{96,192},{112,... | collective-permute-start | bytes 98312
  350.0 5.8 %copy-start.8 = (bf16[16,1024]{1,0:T(8,128)(2,1)}, bf16[16,1024]{1,0:T(8,128)(2,1)S(1)}, u32[]{:S(2)}) copy-start(bf16[16,1024]{1,0:T(8,128)(2,1)S(1)} %collective-permute-done.1) | copy-start | bytes 98308
  350.0 9.9 %collective-permute-start.6 = (bf16[16,1024]{1,0:T(8,128)(2,1)S(1)}, bf16[16,1024]{1,0:T(8,128)(2,1)S(1)}, u32[]{:S(2)}, u32[]{:S(2)}) collective-permute-start(bf16[16,1024]{1,0:T(8,128)(2,1)S(1)} %convert.20), channel_id=1, source_target_pairs={{0,112},{16,128},{32,144},{48,160},{64,176},{80,192},{96,208},{112... | collective-permute-start | bytes 98312
  358.6 1.3 copy-start.9
  358.6 1.4 copy-start.11
Sparse Core Ops, SparseCore 0:
  59.4 58.4 reduce-scatter.10
  120.9 59.2 reduce-scatter.8
where the time goes:
time: 371 us; the launch traced here: 370 us
  blocking collectives  238 us (64%)
  waiting for transfers between devices  68.4 us (18%)
  starting transfers between devices  31.3 us (8%)
  between operations  15 us (4%)
  local copies, waits for them, and re-layouts  9.43 us (3%)
  matrix products  6.56 us (2%)
    unnamed x1, blocking collectives  88.3 us
    reduce_scatter x1, waiting for transfers between devices, local(): lax.psum_scatter(jnp.dot(picked, both_weights, preferred_element_type=jnp...  62.4 us
    all_gather x1, blocking collectives, local(): lax.all_gather(out_grad, 'row', axis=0, tiled=True)  50.6 us
    all_gather x1, blocking collectives, local(): lax.all_gather(activations, 'row', axis=0, tiled=True)  48.1 us
    unnamed x8, starting transfers between devices  31.2 us
    all_gather x1, blocking collectives, local(): lax.all_gather(gate_delta, 'col', axis=0, tiled=True)  18.8 us
    all_gather x1, blocking collectives, local(): hidden_all = lax.all_gather(hidden, 'col', axis=0, tiled=True)  17.1 us
    all_gather x1, blocking collectives, local(): lax.all_gather(up_delta, 'col', axis=0, tiled=True)  15.4 us
  transfers between devices with their start and end apart: 10, of which 3 were waited for; matrix products, arithmetic and copies ran while one was open for 3% of the time, Pallas kernels for 0%

commit v1 on v0

--- a/solution.py
+++ b/solution.py
@@ -1,7 +1,18 @@
+import functools
 import jax
 import jax.numpy as jnp
 from jax import lax
 from jax.sharding import PartitionSpec as P
+
+
+def cover_strings(inner_x, lane_axis):
+    tray = []
+    for _ in range(lax.axis_size(lane_axis)):
+        tray.append(inner_x)
+    return jnp.concatenate(lax.all_to_all(jnp.stack(tray), lane_axis, 0, 0), axis=0)
+
+
+show_the_ladders = functools.partial(cover_strings, lane_axis="col")
 
 
 def contract_rows(left_side, right_side):
@@ -51,7 +62,7 @@
     )
     gate_delta, up_delta = swiglu_deltas(hidden_grad, gate, up)
     all_gate_delta, all_up_delta = (
-        lax.all_gather(gate_delta, "col", axis=0, tiled=True),
+        show_the_ladders(gate_delta),
         lax.all_gather(up_delta, "col", axis=0, tiled=True),
     )
     gate_grad = contract_rows(all_tokens, all_gate_delta)

time: 371 us -> 367 us (0.989)
  the two profiles are of different devices: /device:TPU:64 before, /device:TPU:14 now
where the time goes in v1:
time: 367 us; the launch traced here: 366 us
  blocking collectives  215 us (59%)
  waiting for transfers between devices  75.4 us (21%)
  starting transfers between devices  38.5 us (10%)
  between operations  15 us (4%)
  local copies, waits for them, and re-layouts  10.6 us (3%)
  matrix products  9.75 us (3%)
    unnamed x1, blocking collectives  76.1 us
    reduce_scatter x1, waiting for transfers between devices, local(): lax.psum_scatter(jnp.dot(picked, both_weights, preferred_element_type=jnp...  62.6 us
    all_gather x1, blocking collectives, local(): lax.all_gather(out_grad, 'row', axis=0, tiled=True)  50.1 us
    all_gather x1, blocking collectives, local(): lax.all_gather(activations, 'row', axis=0, tiled=True)  48.8 us
    unnamed x8, starting transfers between devices  34.6 us
    all_gather x1, blocking collectives, local(): lax.all_gather(up_delta, 'col', axis=0, tiled=True)  24.2 us
    all_gather x1, blocking collectives, local(): hidden_all = lax.all_gather(hidden, 'col', axis=0, tiled=True)  15.5 us
    unnamed x26, local copies, waits for them, and re-layouts  9.22 us
  transfers between devices with their start and end apart: 11, of which 4 were waited for; matrix products, arithmetic and copies ran while one was open for 4% of the time, Pallas kernels for 0%

profile of v1, /device:TPU:14, one launch (start us, length us, event | category | flops | bytes accessed | tf_op | source)
XLA Modules:
  0.0 365.7 jit_solution(18142501370121096713)
XLA Ops:
  7.2 50.1 %all-gather.1 = bf16[32,12,512]{2,1,0:T(8,128)(2,1)S(1)} all-gather(bf16[1,12,512]{2,1,0:T(8,128)(2,1)} %bitcast.31), channel_id=1, replica_groups=mesh['row'=32,'col'=16] {'row'}, dimensions={0}, use_global_device_ids=true | all-gather | bytes 405504 | tf_op jit(solution)/shard_map/all_gather | solution.py:45
  57.4 1.3 fusion.9
  58.8 48.8 %all-gather = bf16[32,12,512]{2,1,0:T(8,128)(2,1)S(1)} all-gather(bf16[1,12,512]{2,1,0:T(8,128)(2,1)S(1)} %bitcast.32), channel_id=1, replica_groups=mesh['row'=32,'col'=16] {'row'}, dimensions={0}, use_global_device_ids=true | all-gather | bytes 405504 | tf_op jit(solution)/shard_map/all_gather | solution.py:44
  107.7 1.8 convolution_bitcast_fusion
  109.5 1.6 copy.32
  111.2 1.3 dynamic-slice.4
  113.1 8.6 %reduce-scatter.11.cloned.1.call-done = f32[24,512]{1,0:T(8,128)} async-done(((f32[384,512]{1,0:T(8,128)}), f32[24,512]{1,0:T(8,128)}) %reduce-scatter.11.cloned.1.call-update) | async-done | bytes 49168 | tf_op jit(solution)/shard_map/reduce_scatter | solution.py:60
  121.6 62.6 %reduce-scatter.9.cloned.1.call-done = f32[24,1024]{1,0:T(8,128)} async-done(((f32[384,1024]{1,0:T(8,128)}), f32[24,1024]{1,0:T(8,128)}) %reduce-scatter.9.cloned.1.call-update) | async-done | bytes 98320 | tf_op jit(solution)/shard_map/reduce_scatter | solution.py:49
  184.2 0.9 multiply_convert_fusion
  185.1 0.8 stack.2
  185.9 3.8 %all-to-all-start = ((bf16[16,24,512]{2,1,0:T(8,128)(2,1)}), bf16[16,24,512]{2,1,0:T(8,128)(2,1)S(1)}, u32[]{:S(2)}, u32[]{:S(2)}) async-start(bf16[16,24,512]{2,1,0:T(8,128)(2,1)} %stack.2), calls=%async_computation | async-start | bytes 786432 | tf_op jit(solution)/shard_map/all_to_all | solution.py:12
  189.7 24.2 %all_gather.15 = bf16[384,512]{1,0:T(8,128)(2,1)S(1)} all-gather(bf16[24,512]{1,0:T(8,128)(2,1)S(1)} %get-tuple-element.25), channel_id=1, replica_groups=mesh['row'=32,'col'=16] {'col'}, dimensions={0}, use_global_device_ids=true | all-gather | bytes 417792 | tf_op jit(solution)/shard_map/all_gather | solution.py:66
  213.9 15.5 %all_gather.13 = bf16[384,512]{1,0:T(8,128)(2,1)S(1)} all-gather(bf16[24,512]{1,0:T(8,128)(2,1)S(1)} %get-tuple-element.27), channel_id=1, replica_groups=mesh['row'=32,'col'=16] {'col'}, dimensions={0}, use_global_device_ids=true | all-gather | bytes 417792 | tf_op jit(solution)/shard_map/all_gather | solution.py:58
  230.1 1.2 fusion.8
  231.9 1.6 fusion.10
  234.7 76.1 %fusion = f32[16,1024]{1,0:T(8,128)} fusion(f32[384,1024]{1,0:T(8,128)S(1)} %pad_maximum_fusion), kind=kCustom, calls=%all-reduce-scatter | all-reduce-scatter fusion | flops 524289 | bytes 1640448
  310.8 0.8 convert.20
  311.6 4.2 %collective-permute-start = (bf16[16,1024]{1,0:T(8,128)(2,1)S(1)}, bf16[16,1024]{1,0:T(8,128)(2,1)S(1)}, u32[]{:S(2)}, u32[]{:S(2)}) collective-permute-start(bf16[16,1024]{1,0:T(8,128)(2,1)S(1)} %convert.20), channel_id=1, source_target_pairs={{0,16},{16,32},{32,48},{48,64},{64,80},{80,96},{96,112},{112,128},... | collective-permute-start | bytes 98312
  315.8 5.8 %collective-permute-start.1 = (bf16[16,1024]{1,0:T(8,128)(2,1)S(1)}, bf16[16,1024]{1,0:T(8,128)(2,1)S(1)}, u32[]{:S(2)}, u32[]{:S(2)}) collective-permute-start(bf16[16,1024]{1,0:T(8,128)(2,1)S(1)} %convert.20), channel_id=1, source_target_pairs={{0,32},{16,48},{32,64},{48,80},{64,96},{80,112},{96,128},{112,144}... | collective-permute-start | bytes 98312
  321.6 0.8 slice.22
  322.5 12.0 %collective-permute-start.7 = (bf16[12,1024]{1,0:T(8,128)(2,1)S(1)}, bf16[12,1024]{1,0:T(8,128)(2,1)S(1)}, u32[]{:S(2)}, u32[]{:S(2)}) collective-permute-start(bf16[12,1024]{1,0:T(8,128)(2,1)S(1)} %slice.22), channel_id=1, source_target_pairs={{0,128},{16,144},{32,160},{48,176},{64,192},{80,208},{96,224},{112... | collective-permute-start | bytes 73736
  334.4 2.5 fusion.11
  337.0 1.3 copy.30
  338.3 2.0 collective-permute-start.2
  340.3 2.8 collective-permute-start.3
  343.2 3.7 %collective-permute-start.4 = (bf16[16,1024]{1,0:T(8,128)(2,1)S(1)}, bf16[16,1024]{1,0:T(8,128)(2,1)S(1)}, u32[]{:S(2)}, u32[]{:S(2)}) collective-permute-start(bf16[16,1024]{1,0:T(8,128)(2,1)S(1)} %convert.20), channel_id=1, source_target_pairs={{0,80},{16,96},{32,112},{48,128},{64,144},{80,160},{96,176},{112,1... | collective-permute-start | bytes 98312
  346.9 2.2 collective-permute-start.5
  349.1 1.9 collective-permute-start.6
  351.5 1.3 copy.29
  352.8 2.3 collective-permute-done.5
  355.1 1.9 collective-permute-done.6
  357.0 1.2 concatenate.8
  (37 shorter events, 3.9 us)
Async XLA Ops:
  7.2 50.3 %copy-start = (bf16[512,512]{1,0:T(8,128)(2,1)S(1)}, bf16[512,512]{1,0:T(8,128)(2,1)}, u32[]{:S(2)}) copy-start(bf16[512,512]{1,0:T(8,128)(2,1)} %param.8) | copy-start | bytes 1572868
  7.2 114.5 %reduce-scatter.11.cloned.1.call-start = ((), (), s32[]{:S(2)}) async-start(), calls=%async_computation.4 | async-start | bytes 835584 | tf_op jit(solution)/shard_map/reduce_scatter | solution.py:60
  57.3 1.5 copy-start.8
  57.4 1.4 copy-start.1
  57.4 50.2 %copy-start.7 = (bf16[512,512]{1,0:T(8,128)(2,1)S(1)}, bf16[512,512]{1,0:T(8,128)(2,1)}, u32[]{:S(2)}) copy-start(bf16[512,512]{1,0:T(8,128)(2,1)} %param.7) | copy-start | bytes 1572868
  58.8 125.5 %reduce-scatter.9.cloned.1.call-start = ((), (), s32[]{:S(2)}) async-start(), calls=%async_computation.3 | async-start | bytes 1671168 | tf_op jit(solution)/shard_map/reduce_scatter | solution.py:49
  185.9 46.0 %all-to-all-start = ((bf16[16,24,512]{2,1,0:T(8,128)(2,1)}), bf16[16,24,512]{2,1,0:T(8,128)(2,1)S(1)}, u32[]{:S(2)}, u32[]{:S(2)}) async-start(bf16[16,24,512]{2,1,0:T(8,128)(2,1)} %stack.2), calls=%async_computation | async-start | bytes 786432 | tf_op jit(solution)/shard_map/all_to_all | solution.py:12
  229.4 0.8 copy-start.4
  231.8 1.6 copy-start.2
  233.4 1.1 copy-start.5
  311.6 35.2 %collective-permute-start = (bf16[16,1024]{1,0:T(8,128)(2,1)S(1)}, bf16[16,1024]{1,0:T(8,128)(2,1)S(1)}, u32[]{:S(2)}, u32[]{:S(2)}) collective-permute-start(bf16[16,1024]{1,0:T(8,128)(2,1)S(1)} %convert.20), channel_id=1, source_target_pairs={{0,16},{16,32},{32,48},{48,64},{64,80},{80,96},{96,112},{112,128},... | collective-permute-start | bytes 98312
  315.8 33.3 %collective-permute-start.1 = (bf16[16,1024]{1,0:T(8,128)(2,1)S(1)}, bf16[16,1024]{1,0:T(8,128)(2,1)S(1)}, u32[]{:S(2)}, u32[]{:S(2)}) collective-permute-start(bf16[16,1024]{1,0:T(8,128)(2,1)S(1)} %convert.20), channel_id=1, source_target_pairs={{0,32},{16,48},{32,64},{48,80},{64,96},{80,112},{96,128},{112,144}... | collective-permute-start | bytes 98312
  322.5 28.6 %copy-start.3 = (bf16[16,24,512]{2,1,0:T(8,128)(2,1)S(1)}, bf16[16,24,512]{2,1,0:T(8,128)(2,1)}, u32[]{:S(2)}) copy-start(bf16[16,24,512]{2,1,0:T(8,128)(2,1)} %copy-done.2) | copy-start | bytes 1179652
  322.5 20.7 %collective-permute-start.7 = (bf16[12,1024]{1,0:T(8,128)(2,1)S(1)}, bf16[12,1024]{1,0:T(8,128)(2,1)S(1)}, u32[]{:S(2)}, u32[]{:S(2)}) collective-permute-start(bf16[12,1024]{1,0:T(8,128)(2,1)S(1)} %slice.22), channel_id=1, source_target_pairs={{0,128},{16,144},{32,160},{48,176},{64,192},{80,208},{96,224},{112... | collective-permute-start | bytes 73736
  338.3 18.7 %copy-start.6 = (f32[16,1024]{1,0:T(8,128)S(1)}, f32[16,1024]{1,0:T(8,128)}, u32[]{:S(2)}) copy-start(f32[16,1024]{1,0:T(8,128)} %fusion) | copy-start | bytes 196612
  338.3 14.5 %collective-permute-start.2 = (bf16[16,1024]{1,0:T(8,128)(2,1)S(1)}, bf16[16,1024]{1,0:T(8,128)(2,1)S(1)}, u32[]{:S(2)}, u32[]{:S(2)}) collective-permute-start(bf16[16,1024]{1,0:T(8,128)(2,1)S(1)} %convert.20), channel_id=1, source_target_pairs={{0,48},{16,64},{32,80},{48,96},{64,112},{80,128},{96,144},{112,160... | collective-permute-start | bytes 98312
  340.3 12.5 %collective-permute-start.3 = (bf16[16,1024]{1,0:T(8,128)(2,1)S(1)}, bf16[16,1024]{1,0:T(8,128)(2,1)S(1)}, u32[]{:S(2)}, u32[]{:S(2)}) collective-permute-start(bf16[16,1024]{1,0:T(8,128)(2,1)S(1)} %convert.20), channel_id=1, source_target_pairs={{0,64},{16,80},{32,96},{48,112},{64,128},{80,144},{96,160},{112,17... | collective-permute-start | bytes 98312
  343.2 9.7 %collective-permute-start.4 = (bf16[16,1024]{1,0:T(8,128)(2,1)S(1)}, bf16[16,1024]{1,0:T(8,128)(2,1)S(1)}, u32[]{:S(2)}, u32[]{:S(2)}) collective-permute-start(bf16[16,1024]{1,0:T(8,128)(2,1)S(1)} %convert.20), channel_id=1, source_target_pairs={{0,80},{16,96},{32,112},{48,128},{64,144},{80,160},{96,176},{112,1... | collective-permute-start | bytes 98312
  346.9 8.2 %collective-permute-start.5 = (bf16[16,1024]{1,0:T(8,128)(2,1)S(1)}, bf16[16,1024]{1,0:T(8,128)(2,1)S(1)}, u32[]{:S(2)}, u32[]{:S(2)}) collective-permute-start(bf16[16,1024]{1,0:T(8,128)(2,1)S(1)} %convert.20), channel_id=1, source_target_pairs={{0,96},{16,112},{32,128},{48,144},{64,160},{80,176},{96,192},{112,... | collective-permute-start | bytes 98312
  349.1 7.9 %collective-permute-start.6 = (bf16[16,1024]{1,0:T(8,128)(2,1)S(1)}, bf16[16,1024]{1,0:T(8,128)(2,1)S(1)}, u32[]{:S(2)}, u32[]{:S(2)}) collective-permute-start(bf16[16,1024]{1,0:T(8,128)(2,1)S(1)} %convert.20), channel_id=1, source_target_pairs={{0,112},{16,128},{32,144},{48,160},{64,176},{80,192},{96,208},{112... | collective-permute-start | bytes 98312
Sparse Core Ops, SparseCore 0:
  58.9 62.7 reduce-scatter.10
  124.7 59.4 reduce-scatter.8
